TPU v7x, 128 devices: a whole 4x4x4 slice. The times are simulated.
128 devices in a mesh: dp: 4 (over x), seq: 32 (over z, y, core).
Axes of the slice: x: 4, y: 4, z: 4, core: 2. Of those that a mesh axis runs over, the one named last changes fastest.
Arguments:
- conv_input: bfloat16 [16384, 5376], P(('dp', 'seq')), may hold values from -6 to 6
- doc_start: int32 [16384], P(('dp', 'seq')), may hold values 0 or 1
- conv_weight: float32 [4, 5376], replicated, may hold values from -3 to 3
- conv_bias: float32 [5376], replicated, may hold values from -0.5 to 0.5
- dt_raw: float32 [16384, 80], P(('dp', 'seq')), may hold values from -3 to 3
- dt_bias: float32 [80], replicated, may hold values from -5.5 to -4.2
- a_log: float32 [80], replicated, may hold values from -9 to 2, as said below
- skip_gain: float32 [80], replicated, may hold values from 0.5 to 1.5
- cotangent: bfloat16 [16384, 5120], P(('dp', 'seq')), may hold values from -6 to 6
Outputs:
- ssm_output: bfloat16 [16384, 5120], P(('dp', 'seq'))
- grad_input: bfloat16 [16384, 5376], P(('dp', 'seq'))
- grad_conv_weight: float32 [4, 5376], replicated
- grad_conv_bias: float32 [5376], replicated
- grad_dt_bias: float32 [80], replicated
- grad_a_log: float32 [80], replicated
- grad_skip_gain: float32 [80], replicated
Inputs may be any that keep to these rules, and one draw needn't show every extreme that they name: `doc_start`: 1 marks the first token of a document; documents may cross shard boundaries. One value per head; exp(a_log) lies between 25 / 4096 and 4.2, so that the per-token decay rates exp(a_log) * steps_dt run from under 1 / 4096 to about 1.1.
All inputs are finite; a program needn't handle non-finite values.
Results may differ from a plain program's by a relative error of at most 0.00115.
Values may be sent and summed in bfloat16 or wider, within the bound.
A program may use at most 320 MiB of HBM per device.

v0:
```python
import jax
import jax.numpy as jnp
from jax import lax
from jax.sharding import PartitionSpec as P

HEADS = 80
HEAD_DIM = 64
STATE = 128
CONV = 4
BLOCK = 64
INNER = 5120
exact_mode = lax.Precision.HIGHEST


def from_behind(array, axis, by):
    size = lax.axis_size(axis)
    pairs = [(i, i + by) for i in range(size) if 0 <= i + by < size]
    return lax.ppermute(array, axis, pairs)


def prefix(array, axis, combine, identity, reverse):
    size, place = (lax.axis_size(axis), lax.axis_index(axis))
    everything = jax.tree.map(lambda part: lax.all_gather(part, axis), array)
    start = jax.tree.map(
        lambda part, zero: jnp.broadcast_to(jnp.asarray(zero, part.dtype), part.shape),
        array,
        identity,
    )

    def step(k, before):
        at = size - 1 - k if reverse else k
        reached = at > place if reverse else at < place
        new = combine(before, jax.tree.map(lambda part: part[at], everything))
        return jax.tree.map(lambda a, b: jnp.where(reached, a, b), new, before)

    return lax.fori_loop(0, size, step, start)


def prepare_inputs(
    tail_rows, conv_input, doc_start, conv_weight, conv_bias, dt_raw, dt_bias, a_log
):
    row_count = conv_input.shape[0]
    extended = jnp.concatenate([tail_rows, conv_input], axis=0)
    resets = doc_start.astype(jnp.float32)
    segment = jnp.cumsum(resets)
    padded = jnp.concatenate([jnp.zeros((CONV - 1,), jnp.float32), segment])
    convolved = conv_bias[None, :] + conv_weight[CONV - 1][None, :] * extended[CONV - 1 :]
    for offset in range(1, CONV):
        first_row = CONV - 1 - offset
        tap_valid = (padded[first_row : first_row + row_count] == segment).astype(jnp.float32)
        convolved = (
            convolved
            + conv_weight[first_row][None, :]
            * extended[first_row : first_row + row_count]
            * tap_valid[:, None]
        )
    activated = jax.nn.silu(convolved)
    values_x = activated[:, :INNER].reshape(row_count, HEADS, HEAD_DIM)
    keys_b = activated[:, INNER : INNER + STATE]
    reads_c = activated[:, INNER + STATE :]
    steps_dt = jax.nn.softplus(dt_raw + dt_bias[None, :])
    log_decay = -jnp.exp(a_log)[None, :] * steps_dt
    return (values_x, keys_b, reads_c, steps_dt, log_decay)


def scan_block(carry, block_data):
    carry_state, skip_gain = carry
    values_x, keys_b, reads_c, steps_dt, log_decay, resets = block_data
    length = values_x.shape[0]
    segment = jnp.cumsum(resets)
    running = jnp.cumsum(log_decay, axis=0)
    positions = jnp.arange(length)
    causal = (positions[:, None] >= positions[None, :]) & (segment[:, None] == segment[None, :])
    spread_log = running.T[:, :, None] - running.T[:, None, :]
    within = jnp.where(causal[None], jnp.exp(jnp.where(causal[None], spread_log, 0.0)), 0.0)
    scores = jnp.dot(reads_c, keys_b.T, precision=exact_mode)
    weights = within * scores[None] * steps_dt.T[:, None, :]
    output = jnp.einsum("hts,shp->thp", weights, values_x, precision=exact_mode)
    untouched = (segment == 0).astype(running.dtype)
    entry_weight = jnp.exp(running) * untouched[:, None]
    output = (
        output
        + jnp.einsum("tn,hpn->thp", reads_c, carry_state, precision=exact_mode)
        * entry_weight[:, :, None]
    )
    output = output + skip_gain[None, :, None] * values_x
    last_segment = (segment == segment[length - 1]).astype(running.dtype)
    leave_weight = (
        jnp.exp(running[length - 1][None, :] - running) * last_segment[:, None] * steps_dt
    )
    through = jnp.exp(running[length - 1]) * untouched[length - 1]
    added = jnp.einsum(
        "shp,sn->hpn", leave_weight[:, :, None] * values_x, keys_b, precision=exact_mode
    )
    carry_state = carry_state * through[:, None, None] + added
    return ((carry_state, skip_gain), output)


def chain_blocks(values_x, keys_b, reads_c, steps_dt, log_decay, resets, skip_gain, start_state):
    row_count = values_x.shape[0]
    block_count = row_count // BLOCK
    pieces = tuple(
        (
            member.reshape((block_count, BLOCK) + member.shape[1:])
            for member in (values_x, keys_b, reads_c, steps_dt, log_decay, resets)
        )
    )
    stepper = jax.checkpoint(scan_block)
    (final_state, _), outputs = lax.scan(stepper, (start_state, skip_gain), pieces)
    return (outputs.reshape(row_count, INNER), final_state)


def join_states(earlier, later):
    return (earlier[0] * later[0], later[0][:, None, None] * earlier[1] + later[1])


def on_device(
    conv_input, doc_start, conv_weight, conv_bias, dt_raw, dt_bias, a_log, skip_gain, cotangent
):
    row_count = conv_input.shape[0]
    resets = doc_start.astype(jnp.float32)
    after = jnp.concatenate([1.0 - resets[row_count - CONV + 2 :], jnp.ones((1,), jnp.float32)])
    keep_rows = jnp.flip(jnp.cumprod(jnp.flip(after)))
    tail_out = conv_input[row_count - CONV + 1 :] * keep_rows[:, None].astype(jnp.bfloat16)
    tail_in = from_behind(tail_out, "seq", 1)

    def prepare_local(tail_rows, rows_value, weight_value, bias_value, dtb_value, alog_value):
        return prepare_inputs(
            tail_rows,
            rows_value,
            doc_start,
            weight_value,
            bias_value,
            dt_raw,
            dtb_value,
            alog_value,
        )

    prepared, pull_prep = jax.vjp(
        prepare_local,
        tail_in.astype(jnp.float32),
        conv_input.astype(jnp.float32),
        conv_weight,
        conv_bias,
        dt_bias,
        a_log,
    )
    values_x, keys_b, reads_c, steps_dt, log_decay = prepared
    zero_state = jnp.zeros((HEADS, HEAD_DIM, STATE), jnp.float32)

    def local_chain(x_value, b_value, c_value, dt_value, decay_value, gain_value):
        return chain_blocks(
            x_value, b_value, c_value, dt_value, decay_value, resets, gain_value, zero_state
        )

    (local_out, local_state), pull_chain = jax.vjp(
        local_chain, values_x, keys_b, reads_c, steps_dt, log_decay, skip_gain
    )

    def entering(decay_value):
        running = jnp.cumsum(decay_value, axis=0)
        untouched = (jnp.cumsum(resets) == 0).astype(running.dtype)
        return (
            jnp.exp(running) * untouched[:, None],
            jnp.exp(running[row_count - 1]) * untouched[row_count - 1],
        )

    entry_weight, through = entering(log_decay)
    upstream = cotangent.astype(jnp.float32)
    upstream_heads = upstream.reshape(row_count, HEADS, HEAD_DIM)
    adjoint_local = jnp.einsum(
        "thp,tn->hpn", upstream_heads * entry_weight[:, :, None], reads_c, precision=exact_mode
    )
    identity = (jnp.ones((HEADS,), jnp.float32), jnp.zeros((HEADS, HEAD_DIM, STATE), jnp.float32))
    incoming = prefix((through, local_state), "seq", join_states, identity, False)[1]
    adjoint_end = prefix((through, adjoint_local), "seq", join_states, identity, True)[1]

    def carried(c_value, decay_value):
        weight_in, through_in = entering(decay_value)
        added = (
            jnp.einsum("tn,hpn->thp", c_value, incoming, precision=exact_mode)
            * weight_in[:, :, None]
        )
        return (added.reshape(row_count, INNER), through_in[:, None, None] * incoming)

    (carried_out, _), pull_carried = jax.vjp(carried, reads_c, log_decay)
    output = (local_out + carried_out).astype(jnp.bfloat16)
    grad_x, grad_b, grad_c, grad_dt, grad_decay, grad_gain = pull_chain((upstream, adjoint_end))
    grad_c_extra, grad_decay_extra = pull_carried((upstream, adjoint_end))
    grad_tail, grad_rows, grad_weight, grad_bias, grad_dtb, grad_alog = pull_prep(
        (grad_x, grad_b, grad_c + grad_c_extra, grad_dt, grad_decay + grad_decay_extra)
    )
    returned = from_behind(grad_tail, "seq", -1)
    grad_rows = jnp.concatenate(
        [
            grad_rows[: row_count - CONV + 1],
            grad_rows[row_count - CONV + 1 :] + returned * keep_rows[:, None],
        ],
        axis=0,
    )
    summed = lax.psum((grad_weight, grad_bias, grad_dtb, grad_alog, grad_gain), ("dp", "seq"))
    scale = float(lax.axis_size("dp") * lax.axis_size("seq") * row_count) ** (-0.5)
    return (
        output,
        grad_rows.astype(jnp.bfloat16),
        summed[0] * scale,
        summed[1] * scale,
        summed[2] * scale,
        summed[3] * scale,
        summed[4] * scale,
    )


def solution(mesh):
    return jax.shard_map(
        on_device,
        mesh=mesh,
        in_specs=(
            P(("dp", "seq"), None),
            P(("dp", "seq")),
            P(),
            P(),
            P(("dp", "seq"), None),
            P(),
            P(),
            P(),
            P(("dp", "seq"), None),
        ),
        out_specs=(P(("dp", "seq"), None), P(("dp", "seq"), None), P(), P(), P(), P(), P()),
        check_vma=False,
    )
```

profile of v0, /device:TPU:1, one launch (start us, length us, event | category | flops | bytes accessed | tf_op | source)
XLA Modules:
  0.0 1133.3 jit_solution(11397604116379961711)
XLA Ops:
  9.4 4.6 collective-permute-start
  21.4 7.5 fusion.100
  31.3 5.1 reshape.509
  36.5 69.3 %while.76 = (s32[]{:T(128)}, f32[80,64,128]{2,1,0:T(8,128)S(1)}, f32[2,64,80,64]{3,2,1,0:T(8,128)}, f32[2,80,64,128]{3,2,1,0:T(8,128)}, f32[2,80]{1,0:T(2,128)S(...) while((s32[]{:T(128)}, f32[80,64,128]{2,1,0:T(8,128)S(1)}, ...), condition=%wide.region_5.6_spmd.clone, body=%wide.region_2.5_spmd.clone.sunk | while | flops 1271495936 | bytes 43904780 | solution.py:109
  50.0 5.3 multiply_add_fusion.7
  55.8 8.7 fusion.194
  84.6 5.3 multiply_add_fusion.7
  90.4 8.7 fusion.194
  114.3 21.7 %all-gather.2 = f32[32,1,80]{2,1,0:T(1,128)S(1)} all-gather(f32[1,1,80]{2,1,0:T(1,128)S(1)} %multiply_bitcast_fusion), channel_id=1, replica_groups=mesh['dp'=4,'seq'=32] {'seq'}, dimensions={0}, use_global_device_ids=true | all-gather | bytes 10560 | tf_op jit(solution)/shard_map/all_gather | solution.py:23
  136.0 218.2 %all-gather.6.cloned.1.call-done = f32[2560,64,128]{2,1,0:T(8,128)} async-done(((f32[80,64,128]{2,1,0:T(8,128)}), f32[2560,64,128]{2,1,0:T(8,128)}) %all-gather.6.cloned.1.call-update) | async-done | bytes 83886096 | tf_op jit(solution)/shard_map/all_gather | solution.py:23
  354.3 77.1 %while.77 = (s32[]{:T(128)}, f32[80,64,128]{2,1,0:T(8,128)S(1)}, s32[]{:T(128)}, f32[32,80]{1,0:T(8,128)S(1)}, f32[32,80,64,128]{3,2,1,0:T(8,128)}, /*index=5*/s32[]{:T(128)}, s32[]{:T(128)}) while((s32[]{:T(128)}, f32[80,64,128]{2,1,0:T(8,128)S(1)}, s32[]{:T(128)}, f32[32,80]{1,0:T(8,128)S(1)}, f32[32,80,64,128]{3,2,1,0:T(8,128)}, ...), condition=%wide.region_8.9_spmd.clone, body=%wide.region_7.8_spmd.clone.sunk | while | flops 2621444 | bytes 7865393 | solution.py:36
  431.3 8.7 multiply_reduce_fusion.10
  441.5 5.1 fusion.101
  446.7 6.0 reshape.542
  452.7 8.1 copy.125
  460.8 6.5 copy.124
  467.3 5.4 reshape.512
  472.7 4.2 copy.118
  484.9 205.6 %all-gather.8.cloned.1.call-done = f32[2560,64,128]{2,1,0:T(8,128)} async-done(((f32[80,64,128]{2,1,0:T(8,128)}), f32[2560,64,128]{2,1,0:T(8,128)}) %all-gather.8.cloned.1.call-update) | async-done | bytes 83886096 | tf_op jit(solution)/shard_map/all_gather | solution.py:23
  690.5 77.1 %while.78 = (s32[]{:T(128)}, f32[80,64,128]{2,1,0:T(8,128)S(1)}, s32[]{:T(128)}, f32[32,80]{1,0:T(8,128)S(1)}, f32[32,80,64,128]{3,2,1,0:T(8,128)}, /*index=5*/s32[]{:T(128)}, s32[]{:T(128)}, s32[]{:T(128)}, s32[]{:T(128)}) while((s32[]{:T(128)}, f32[80,64,128]{2,1,0:T(8,128)S(1)}, s32[]{:T(128)}, f32[32,80]{1,0:T(8,128)S(1)}, ...), condition=%wide.region_10.11_spmd.clone, body=%wide.region_9.10_spmd.clone.sunk | while | flops 2621448 | bytes 7865455 | solution.py:36
  772.6 176.0 %while.79 = (s32[]{:T(128)}, f32[80,64,128]{2,1,0:T(8,128)}, f32[80]{0:T(128)S(1)}, f32[2,64,80,64]{2,1,3,0:T(8,128)}, f32[2,64,128]{2,1,0:T(8,128)S(1)}, /*inde...) while((s32[]{:T(128)}, f32[80,64,128]{2,1,0:T(8,128)}, ...), condition=%wide.region_24.25_spmd.clone, body=%wide.region_11.24_spmd.clone.sunk | while | flops 3052656640 | bytes 114250048 | solution.py:109
  784.3 4.6 copy.230
  788.9 8.2 fusion.220
  797.3 9.1 multiply_reduce_fusion.17
  811.5 9.6 multiply_reduce_fusion.16
  821.3 4.1 fusion.223
  825.3 4.5 copy.225
  830.5 6.4 multiply_add_fusion.8
  836.9 6.5 fusion.219
  843.4 4.1 copy.229
  847.5 4.5 bitcast_dynamic-update-slice_fusion.7
  852.3 3.9 fusion.225
  868.3 4.7 copy.230
  873.0 8.2 fusion.220
  881.4 9.1 multiply_reduce_fusion.17
  895.6 9.6 multiply_reduce_fusion.16
  905.4 4.1 fusion.223
  909.5 4.7 copy.225
  914.8 6.4 multiply_add_fusion.8
  921.2 6.5 fusion.219
  931.6 4.5 bitcast_dynamic-update-slice_fusion.7
  936.3 3.9 fusion.225
  948.6 6.1 copy.127
  954.8 5.5 reshape.518
  960.3 7.3 fusion.110
  967.7 5.5 multiply_reduce_fusion.9
  986.6 66.0 %all-reduce.15 = (f32[5376]{0:T(1024)S(1)}, f32[80]{0:T(128)S(1)}, f32[80]{0:T(128)S(1)}, f32[80]{0:T(128)S(1)}) all-reduce(f32[5376]{0:T(1024)S(1)} %get-tuple-element.978, f32[80]{0:T(128)S(1)} %get-tuple-element.981, f32[80]{0:T(128)S(1)} %negate_multiply_fusion, ...), channel_id=1, replica_groups=mesh['dp'=4,'seq'=32] {'dp','seq'}, use_global_device_ids=true, to_apply=%region_31.32 | all-reduce | flops 5616 | bytes 44928 | tf_op jit(solution)/shard_map/psum | solution.py:201
  1057.0 65.2 %all-reduce.18.cloned.1.call-done = f32[4,5376]{1,0:T(4,128)} async-done(((f32[4,5376]{1,0:T(4,128)}), f32[4,5376]{1,0:T(4,128)}) %all-reduce.18.cloned.1.call-update) | async-done | bytes 86032 | tf_op jit(solution)/shard_map/psum | solution.py:201
  (441 shorter events, 289.2 us)
Async XLA Ops:
  7.2 14.3 %copy-start.37 = (f32[5376]{0:T(1024)S(1)}, f32[5376]{0:T(1024)}, u32[]{:S(2)}) copy-start(f32[5376]{0:T(1024)} %param.20) | copy-start | bytes 64516
  7.2 347.1 %all-gather.6.cloned.1.call-start = ((), (), s32[]{:S(2)}) async-start(), calls=%async_computation.1 | async-start | bytes 86507520 | tf_op jit(solution)/shard_map/all_gather | solution.py:23
  8.4 7.2 copy-start.50
  9.4 12.0 %collective-permute-start = (bf16[3,5376]{1,0:T(4,128)(2,1)S(1)}, bf16[3,5376]{1,0:T(4,128)(2,1)S(1)}, u32[]{:S(2)}, u32[]{:S(2)}) collective-permute-start(bf16[3,5376]{1,0:T(4,128)(2,1)S(1)} %slice_multiply_fusion), channel_id=1, source_target_pairs={{0,1},{1,2},{2,3},{3,4},{4,5},{5,6},{6,7},{7,8},{8,9},{9,10},{10,1... | collective-permute-start | bytes 96776 | tf_op jit(solution)/shard_map/ppermute | solution.py:18
  14.9 14.0 %copy-start.26 = (f32[128,80]{1,0:T(8,128)}, f32[128,80]{1,0:T(8,128)S(1)}, u32[]{:S(2)}) copy-start(f32[128,80]{1,0:T(8,128)S(1)} %copy.111) | copy-start | bytes 122884
  16.1 12.8 %copy-start.39 = (f32[128]{0:T(128)}, f32[128]{0:T(128)S(1)}, u32[]{:S(2)}) copy-start(f32[128]{0:T(128)S(1)} %get-tuple-element.1103) | copy-start | bytes 1540
  16.1 12.8 %copy-start.41 = (f32[128]{0:T(128)}, f32[128]{0:T(128)S(1)}, u32[]{:S(2)}) copy-start(f32[128]{0:T(128)S(1)} %get-tuple-element.1104) | copy-start | bytes 1540
  16.1 12.9 %copy-start.43 = (f32[128]{0:T(128)}, f32[128]{0:T(128)S(1)}, u32[]{:S(2)}) copy-start(f32[128]{0:T(128)S(1)} %get-tuple-element.1105) | copy-start | bytes 1540
  16.1 97.4 %copy-start.45 = (f32[128]{0:T(128)}, f32[128]{0:T(128)S(1)}, u32[]{:S(2)}) copy-start(f32[128]{0:T(128)S(1)} %get-tuple-element.1102) | copy-start | bytes 1540
  18.1 10.8 copy-start.29
  18.1 10.8 copy-start.31
  18.2 10.8 copy-start.33
  18.2 10.8 copy-start.35
  21.4 7.6 copy-start.22
  31.3 5.2 copy-start.38
  107.3 583.2 %all-gather.8.cloned.1.call-start = ((), (), s32[]{:S(2)}) async-start(), calls=%async_computation.2 | async-start | bytes 86507520 | tf_op jit(solution)/shard_map/all_gather | solution.py:23
  112.9 241.4 %copy-start.24 = (f32[128,80]{1,0:T(8,128)}, f32[128,80]{1,0:T(8,128)S(1)}, u32[]{:S(2)}) copy-start(f32[128,80]{1,0:T(8,128)S(1)} %reduce_window_sum.84) | copy-start | bytes 122884
  431.3 8.7 copy-start.5
  446.6 675.6 %all-reduce.18.cloned.1.call-start = ((), (), s32[]{:S(2)}) async-start(), calls=%async_computation | async-start | bytes 172032 | tf_op jit(solution)/shard_map/psum | solution.py:201
  797.3 9.1 copy-start
  806.4 5.2 copy-start.2
  830.5 6.4 copy-start.10
  847.5 4.8 copy-start.1
  847.5 4.8 copy-start.4
  881.3 9.1 copy-start
  890.4 5.2 copy-start.2
  914.8 6.4 copy-start.10
  931.5 4.8 copy-start.1
  954.8 5.5 copy-start.6
  954.8 12.9 %copy-start.23 = (f32[3,5376]{1,0:T(4,128)S(1)}, f32[3,5376]{1,0:T(4,128)}, u32[]{:S(2)}) copy-start(f32[3,5376]{1,0:T(4,128)} %copy-done.22) | copy-start | bytes 193540
  960.3 7.4 copy-start.17
  960.3 7.4 copy-start.20
  960.3 7.4 copy-start.40
  960.3 7.4 copy-start.42
  960.3 7.4 copy-start.44
  967.7 5.6 copy-start.30
  967.7 5.6 copy-start.32
  967.7 5.6 copy-start.34
  967.7 5.6 copy-start.36
  980.3 5.0 copy-start.28
  980.3 5.0 copy-start.46
  980.3 6.2 copy-start.27
  980.3 6.2 copy-start.47
  980.3 6.2 copy-start.49
  980.3 6.3 copy-start.52
  981.0 142.8 %copy-start.13 = (f32[128,5376]{1,0:T(8,128)S(1)}, f32[128,5376]{1,0:T(8,128)}, u32[]{:S(2)}) copy-start(f32[128,5376]{1,0:T(8,128)} %copy-done.12) | copy-start | bytes 8257540
  981.0 142.8 %copy-start.51 = (f32[3]{0:T(128)S(1)}, f32[3]{0:T(128)}, u32[]{:S(2)}) copy-start(f32[3]{0:T(128)} %copy-done.50) | copy-start | bytes 40
  981.0 142.8 %collective-permute-start.1 = (f32[3,5376]{1,0:T(4,128)S(1)}, f32[3,5376]{1,0:T(4,128)S(1)}, u32[]{:S(2)}, u32[]{:S(2)}) collective-permute-start(f32[3,5376]{1,0:T(4,128)S(1)} %pad_add_fusion.1), channel_id=1, source_target_pairs={{1,0},{2,1},{3,2},{4,3},{5,4},{6,5},{7,6},{8,7},{9,8},{10,9},{11,1... | collective-permute-start | bytes 193544 | tf_op jit(solution)/shard_map/ppermute | solution.py:18
  (17 other events, 46.8 us)
Sparse Core Ops, SparseCore 0:
  107.4 246.8 all-gather.5
  446.8 243.7 all-gather.7
  984.7 137.4 all-reduce.17
where the time goes:
time: 1140 us; the launch traced here: 1130 us
  waiting for transfers between devices  489 us (43%)
  other arithmetic  218 us (19%)
  matrix products  153 us (13%)
  local copies, waits for them, and re-layouts  151 us (13%)
  blocking collectives  87.7 us (8%)
  between operations  14.8 us (1%)
  loops' own time  12 us (1%)
    all_gather x2, waiting for transfers between devices, prefix(): everything = jax.tree.map(lambda part: lax.all_gather(part, axis), array)  424 us
    select_n x64, other arithmetic, step(): return jax.tree.map(lambda a, b: jnp.where(reached, a, b), new, before)  151 us
    psum x1, blocking collectives, on_device(): lax.psum((grad_weight, grad_bias, grad_dtb, grad_alog, grad_gain), ('dp',...  66 us
    psum x1, waiting for transfers between devices, on_device(): lax.psum((grad_weight, grad_bias, grad_dtb, grad_alog, grad_gain), ('dp',...  65.2 us
    dot_general x6, matrix products, scan_block(): output = jnp.einsum('hts,shp->thp', weights, values_x, precision=exact_mode)  46.7 us
    dot_general x8, matrix products, scan_block(): jnp.einsum('tn,hpn->thp', reads_c, carry_state, precision=exact_mode)  46.1 us
    dot_general x6, matrix products, scan_block(): jnp.einsum('shp,sn->hpn', leave_weight[:, :, None] * values_x, keys_b, pr...  37.8 us
    unnamed x97, local copies, waits for them, and re-layouts  28 us
  transfers between devices with their start and end apart: 5, of which 3 were waited for; matrix products, arithmetic and copies ran while one was open for 5% of the time, Pallas kernels for 0%

commit v1 on v0

--- a/solution.py
+++ b/solution.py
@@ -198,7 +198,9 @@
         ],
         axis=0,
     )
-    summed = lax.psum((grad_weight, grad_bias, grad_dtb, grad_alog, grad_gain), ("dp", "seq"))
+    summed = lax.psum(
+        lax.psum((grad_weight, grad_bias, grad_dtb, grad_alog, grad_gain), "dp"), "seq"
+    )
     scale = float(lax.axis_size("dp") * lax.axis_size("seq") * row_count) ** (-0.5)
     return (
         output,

time: 1140 us -> 1280 us (1.12)
  waiting for transfers between devices: 489 us -> 562 us
  blocking collectives: 87.7 us -> 156 us
    psum x1 -> x2, waiting for transfers between devices: 65.2 us -> 138 us  [the longest x1 101 us: on_device(): lax.psum(lax.psum((grad_weight, grad_bias, grad_dtb, grad_alog, grad_gain...]
    psum x1 -> x2, blocking collectives: 66 us -> 135 us  [the longest x1 121 us: on_device(): lax.psum(lax.psum((grad_weight, grad_bias, grad_dtb, grad_alog, grad_gain...]
    unnamed x97 -> x95, local copies, waits for them, and re-layouts: 28 us -> 27.7 us
  transfers between devices with their start and end apart: 5 -> 6, of which waited for: 3 -> 4; matrix products, arithmetic and copies ran while one was open for 5% -> 5% of each run, Pallas kernels for 0% -> 0%
where the time goes in v1:
time: 1280 us
  waiting for transfers between devices  562 us (44%)
  other arithmetic  219 us (17%)
  blocking collectives  156 us (12%)
  matrix products  153 us (12%)
  local copies, waits for them, and re-layouts  151 us (12%)
  between operations  14.8 us (1%)
    all_gather x2, waiting for transfers between devices, prefix(): everything = jax.tree.map(lambda part: lax.all_gather(part, axis), array)  424 us
    select_n x64, other arithmetic, step(): return jax.tree.map(lambda a, b: jnp.where(reached, a, b), new, before)  151 us
    psum x1, blocking collectives, on_device(): lax.psum(lax.psum((grad_weight, grad_bias, grad_dtb, grad_alog, grad_gain...  121 us
    psum x1, waiting for transfers between devices, on_device(): lax.psum(lax.psum((grad_weight, grad_bias, grad_dtb, grad_alog, grad_gain...  101 us
    dot_general x6, matrix products, scan_block(): output = jnp.einsum('hts,shp->thp', weights, values_x, precision=exact_mode)  46.7 us
    dot_general x8, matrix products, scan_block(): jnp.einsum('tn,hpn->thp', reads_c, carry_state, precision=exact_mode)  46.1 us
    dot_general x6, matrix products, scan_block(): jnp.einsum('shp,sn->hpn', leave_weight[:, :, None] * values_x, keys_b, pr...  37.8 us
    psum x1, waiting for transfers between devices, on_device(): lax.psum((grad_weight, grad_bias, grad_dtb, grad_alog, grad_gain), 'dp')  36.8 us
  transfers between devices with their start and end apart: 6, of which 4 were waited for; matrix products, arithmetic and copies ran while one was open for 5% of the time, Pallas kernels for 0%

profile of v1, /device:TPU:1, one launch (start us, length us, event | category | flops | bytes accessed | tf_op | source)
XLA Modules:
  0.0 1275.4 jit_solution(3335038050490632153)
XLA Ops:
  9.4 4.6 collective-permute-start
  21.4 7.5 fusion.100
  31.3 5.1 reshape.509
  36.5 69.3 %while.76 = (s32[]{:T(128)}, f32[80,64,128]{2,1,0:T(8,128)S(1)}, f32[2,64,80,64]{3,2,1,0:T(8,128)}, f32[2,80,64,128]{3,2,1,0:T(8,128)}, f32[2,80]{1,0:T(2,128)S(...) while((s32[]{:T(128)}, f32[80,64,128]{2,1,0:T(8,128)S(1)}, ...), condition=%wide.region_5.6_spmd.clone, body=%wide.region_2.5_spmd.clone.sunk | while | flops 1271495936 | bytes 43904780 | solution.py:109
  50.0 5.3 multiply_add_fusion.7
  55.8 8.7 fusion.194
  84.6 5.3 multiply_add_fusion.7
  90.4 8.7 fusion.194
  114.3 21.7 %all-gather.2 = f32[32,1,80]{2,1,0:T(1,128)S(1)} all-gather(f32[1,1,80]{2,1,0:T(1,128)S(1)} %multiply_bitcast_fusion), channel_id=1, replica_groups=mesh['dp'=4,'seq'=32] {'seq'}, dimensions={0}, use_global_device_ids=true | all-gather | bytes 10560 | tf_op jit(solution)/shard_map/all_gather | solution.py:23
  136.0 218.2 %all-gather.6.cloned.1.call-done = f32[2560,64,128]{2,1,0:T(8,128)} async-done(((f32[80,64,128]{2,1,0:T(8,128)}), f32[2560,64,128]{2,1,0:T(8,128)}) %all-gather.6.cloned.1.call-update) | async-done | bytes 83886096 | tf_op jit(solution)/shard_map/all_gather | solution.py:23
  354.3 77.1 %while.77 = (s32[]{:T(128)}, f32[80,64,128]{2,1,0:T(8,128)S(1)}, s32[]{:T(128)}, f32[32,80]{1,0:T(8,128)S(1)}, f32[32,80,64,128]{3,2,1,0:T(8,128)}, /*index=5*/s32[]{:T(128)}, s32[]{:T(128)}) while((s32[]{:T(128)}, f32[80,64,128]{2,1,0:T(8,128)S(1)}, s32[]{:T(128)}, f32[32,80]{1,0:T(8,128)S(1)}, f32[32,80,64,128]{3,2,1,0:T(8,128)}, ...), condition=%wide.region_8.9_spmd.clone, body=%wide.region_7.8_spmd.clone.sunk | while | flops 2621444 | bytes 7865393 | solution.py:36
  431.3 8.7 multiply_reduce_fusion.10
  441.5 5.1 fusion.101
  446.7 6.0 reshape.542
  452.7 8.1 copy.125
  460.8 6.5 copy.124
  467.3 5.4 reshape.512
  472.7 4.2 copy.118
  484.9 205.6 %all-gather.8.cloned.1.call-done = f32[2560,64,128]{2,1,0:T(8,128)} async-done(((f32[80,64,128]{2,1,0:T(8,128)}), f32[2560,64,128]{2,1,0:T(8,128)}) %all-gather.8.cloned.1.call-update) | async-done | bytes 83886096 | tf_op jit(solution)/shard_map/all_gather | solution.py:23
  690.5 77.1 %while.78 = (s32[]{:T(128)}, f32[80,64,128]{2,1,0:T(8,128)S(1)}, s32[]{:T(128)}, f32[32,80]{1,0:T(8,128)S(1)}, f32[32,80,64,128]{3,2,1,0:T(8,128)}, /*index=5*/s32[]{:T(128)}, s32[]{:T(128)}, s32[]{:T(128)}, s32[]{:T(128)}) while((s32[]{:T(128)}, f32[80,64,128]{2,1,0:T(8,128)S(1)}, s32[]{:T(128)}, f32[32,80]{1,0:T(8,128)S(1)}, ...), condition=%wide.region_10.11_spmd.clone, body=%wide.region_9.10_spmd.clone.sunk | while | flops 2621448 | bytes 7865455 | solution.py:36
  772.6 176.0 %while.79 = (s32[]{:T(128)}, f32[80,64,128]{2,1,0:T(8,128)}, f32[80]{0:T(128)S(1)}, f32[2,64,80,64]{2,1,3,0:T(8,128)}, f32[2,64,128]{2,1,0:T(8,128)S(1)}, /*inde...) while((s32[]{:T(128)}, f32[80,64,128]{2,1,0:T(8,128)}, ...), condition=%wide.region_24.25_spmd.clone, body=%wide.region_11.24_spmd.clone.sunk | while | flops 3052656640 | bytes 114250048 | solution.py:109
  784.3 4.6 copy.230
  788.9 8.2 fusion.220
  797.3 9.1 multiply_reduce_fusion.17
  811.5 9.6 multiply_reduce_fusion.16
  821.3 4.1 fusion.223
  825.3 4.5 copy.225
  830.5 6.4 multiply_add_fusion.8
  836.9 6.5 fusion.219
  843.4 4.1 copy.229
  847.5 4.5 bitcast_dynamic-update-slice_fusion.7
  868.3 4.7 copy.230
  873.0 8.2 fusion.220
  881.4 9.1 multiply_reduce_fusion.17
  895.6 9.6 multiply_reduce_fusion.16
  905.4 4.1 fusion.223
  909.5 4.7 copy.225
  914.8 6.4 multiply_add_fusion.8
  921.2 6.5 fusion.219
  931.6 4.5 bitcast_dynamic-update-slice_fusion.7
  948.6 6.1 copy.127
  954.8 5.5 reshape.518
  960.3 7.3 fusion.110
  967.7 5.5 multiply_reduce_fusion.9
  985.9 13.4 %all-reduce.16 = (f32[5376]{0:T(1024)S(1)}, f32[80]{0:T(128)S(1)}, f32[80]{0:T(128)S(1)}, f32[80]{0:T(128)S(1)}) all-reduce(f32[5376]{0:T(1024)S(1)} %get-tuple-element.978, f32[80]{0:T(128)S(1)} %get-tuple-element.981, f32[80]{0:T(128)S(1)} %negate_multiply_fusion, ...), channel_id=1, replica_groups=mesh['dp'=4,'seq'=32] {'dp'}, use_global_device_ids=true, to_apply=%region_32.33 | all-reduce | flops 5616 | bytes 44928 | tf_op jit(solution)/shard_map/psum | solution.py:202
  999.3 121.1 %all-reduce.15 = (f32[5376]{0:T(1024)S(1)}, f32[80]{0:T(128)S(1)}, f32[80]{0:T(128)S(1)}, f32[80]{0:T(128)S(1)}) all-reduce(f32[5376]{0:T(1024)S(1)} %get-tuple-element.1068, f32[80]{0:T(128)S(1)} %get-tuple-element.1069, f32[80]{0:T(128)S(1)} %get-tuple-element.1070, ...), channel_id=1, replica_groups=mesh['dp'=4,'seq'=32] {'seq'}, use_global_device_ids=true, to_apply=%region_33.34 | all-reduce | flops 5616 | bytes 44928 | tf_op jit(solution)/shard_map/psum | solution.py:201
  1126.8 36.8 %all-reduce.20.cloned.1.call-done = f32[4,5376]{1,0:T(4,128)} async-done(((f32[4,5376]{1,0:T(4,128)}), f32[4,5376]{1,0:T(4,128)}) %all-reduce.20.cloned.1.call-update) | async-done | bytes 86032 | tf_op jit(solution)/shard_map/psum | solution.py:202
  1166.1 100.9 %all-reduce.22.cloned.1.call-done = f32[4,5376]{1,0:T(4,128)} async-done(((f32[4,5376]{1,0:T(4,128)}), f32[4,5376]{1,0:T(4,128)}) %all-reduce.22.cloned.1.call-update) | async-done | bytes 86032 | tf_op jit(solution)/shard_map/psum | solution.py:201
  (443 shorter events, 298.1 us)
Async XLA Ops:
  7.2 14.3 %copy-start.36 = (f32[5376]{0:T(1024)S(1)}, f32[5376]{0:T(1024)}, u32[]{:S(2)}) copy-start(f32[5376]{0:T(1024)} %param.20) | copy-start | bytes 64516
  7.2 347.1 %all-gather.6.cloned.1.call-start = ((), (), s32[]{:S(2)}) async-start(), calls=%async_computation.2 | async-start | bytes 86507520 | tf_op jit(solution)/shard_map/all_gather | solution.py:23
  8.4 7.2 copy-start.49
  9.4 12.0 collective-permute-start
  14.9 14.0 %copy-start.25 = (f32[128,80]{1,0:T(8,128)}, f32[128,80]{1,0:T(8,128)S(1)}, u32[]{:S(2)}) copy-start(f32[128,80]{1,0:T(8,128)S(1)} %copy.111) | copy-start | bytes 122884
  16.1 12.8 %copy-start.38 = (f32[128]{0:T(128)}, f32[128]{0:T(128)S(1)}, u32[]{:S(2)}) copy-start(f32[128]{0:T(128)S(1)} %get-tuple-element.1107) | copy-start | bytes 1540
  16.1 12.8 %copy-start.40 = (f32[128]{0:T(128)}, f32[128]{0:T(128)S(1)}, u32[]{:S(2)}) copy-start(f32[128]{0:T(128)S(1)} %get-tuple-element.1108) | copy-start | bytes 1540
  16.1 12.9 %copy-start.42 = (f32[128]{0:T(128)}, f32[128]{0:T(128)S(1)}, u32[]{:S(2)}) copy-start(f32[128]{0:T(128)S(1)} %get-tuple-element.1109) | copy-start | bytes 1540
  16.1 97.4 %copy-start.44 = (f32[128]{0:T(128)}, f32[128]{0:T(128)S(1)}, u32[]{:S(2)}) copy-start(f32[128]{0:T(128)S(1)} %get-tuple-element.1106) | copy-start | bytes 1540
  18.1 10.8 copy-start.28
  18.1 10.8 copy-start.30
  18.2 10.8 copy-start.32
  18.2 10.8 copy-start.34
  21.4 7.6 copy-start.21
  31.3 5.2 copy-start.37
  107.3 583.2 %all-gather.8.cloned.1.call-start = ((), (), s32[]{:S(2)}) async-start(), calls=%async_computation.3 | async-start | bytes 86507520 | tf_op jit(solution)/shard_map/all_gather | solution.py:23
  112.9 241.4 %copy-start.23 = (f32[128,80]{1,0:T(8,128)}, f32[128,80]{1,0:T(8,128)S(1)}, u32[]{:S(2)}) copy-start(f32[128,80]{1,0:T(8,128)S(1)} %reduce_window_sum.84) | copy-start | bytes 122884
  431.3 8.7 copy-start.5
  446.6 716.9 %all-reduce.20.cloned.1.call-start = ((), (), s32[]{:S(2)}) async-start(), calls=%async_computation | async-start | bytes 172032 | tf_op jit(solution)/shard_map/psum | solution.py:202
  797.3 9.1 copy-start
  806.4 5.2 copy-start.2
  830.5 6.4 copy-start.10
  847.5 4.8 copy-start.1
  847.5 4.8 copy-start.4
  881.3 9.1 copy-start
  890.4 5.2 copy-start.2
  914.8 6.4 copy-start.10
  931.5 4.8 copy-start.1
  931.6 4.8 copy-start.4
  954.8 5.5 copy-start.6
  954.8 12.9 %copy-start.22 = (f32[3,5376]{1,0:T(4,128)S(1)}, f32[3,5376]{1,0:T(4,128)}, u32[]{:S(2)}) copy-start(f32[3,5376]{1,0:T(4,128)} %copy-done.21) | copy-start | bytes 193540
  960.3 7.4 copy-start.17
  960.3 7.4 copy-start.20
  960.3 7.4 copy-start.39
  960.3 7.4 copy-start.41
  960.3 7.4 copy-start.43
  967.7 5.6 copy-start.29
  967.7 5.6 copy-start.31
  967.7 5.6 copy-start.33
  967.7 5.6 copy-start.35
  980.3 5.4 copy-start.26
  980.3 5.4 copy-start.46
  980.3 5.4 copy-start.48
  980.3 5.5 copy-start.51
  981.0 144.6 %copy-start.13 = (f32[128,5376]{1,0:T(8,128)S(1)}, f32[128,5376]{1,0:T(8,128)}, u32[]{:S(2)}) copy-start(f32[128,5376]{1,0:T(8,128)} %copy-done.12) | copy-start | bytes 8257540
  981.0 144.6 %copy-start.50 = (f32[3]{0:T(128)S(1)}, f32[3]{0:T(128)}, u32[]{:S(2)}) copy-start(f32[3]{0:T(128)} %copy-done.49) | copy-start | bytes 40
  981.0 144.6 %collective-permute-start.1 = (f32[3,5376]{1,0:T(4,128)S(1)}, f32[3,5376]{1,0:T(4,128)S(1)}, u32[]{:S(2)}, u32[]{:S(2)}) collective-permute-start(f32[3,5376]{1,0:T(4,128)S(1)} %pad_add_fusion.1), channel_id=1, source_target_pairs={{1,0},{2,1},{3,2},{4,3},{5,4},{6,5},{7,6},{8,7},{9,8},{10,9},{11,1... | collective-permute-start | bytes 193544 | tf_op jit(solution)/shard_map/ppermute | solution.py:18
  1125.5 141.5 %all-reduce.22.cloned.1.call-start = ((), (), s32[]{:S(2)}) async-start(), calls=%async_computation.1 | async-start | bytes 172032 | tf_op jit(solution)/shard_map/psum | solution.py:201
  (17 other events, 48.2 us)
Sparse Core Ops, SparseCore 0:
  107.4 246.8 all-gather.5
  446.8 243.7 all-gather.7
  1125.7 37.8 all-reduce.19
  1167.0 99.9 all-reduce.21
